TPU v7x, 32 devices: a whole 2x2x4 slice. The times are simulated.
32 devices in a mesh: tm: 8 (over z, core), zone: 4 (over y, x).
Axes of the slice: x: 2, y: 2, z: 4, core: 2. Of those that a mesh axis runs over, the one named last changes fastest.
Arguments:
- initial_guess: float32 [15, 3, 4, 1024], P(None, None, 'zone', 'tm'), may hold values from -2.5 to 2.5
- harmonic_loads: float32 [15, 3, 4, 1024], P(None, None, 'zone', 'tm'), may hold values from -12 to 12
- stiffness: bfloat16 [4, 8, 5, 384, 384], P('zone', 'tm'), as said below
- mass_tiles: bfloat16 [4, 8, 384, 384], P('zone', 'tm'), as said below
- block_links: int32 [4, 8, 2], P('zone', 'tm'), may hold values from 0 to 7, as said below
- states: int32 [2048, 4, 1024], P('tm', 'zone'), may hold values from 0 to 2
- preload: float32 [4, 1024], P('zone'), may hold values from 1 to 3
- normal_stiff: float32 [4, 1024], P('zone'), may hold values from 0.5 to 2
- tangent_stiff: float32 [4, 1024], P('zone'), may hold values from 0.3 to 1.5
- friction: float32 [4, 1024], P('zone'), may hold values from 0.2 to 0.8
Outputs:
- coefficients: float32 [15, 3, 4, 1024], P(None, None, 'zone', 'tm')
- residual: float32 [15, 3, 4, 1024], P(None, None, 'zone', 'tm')
Inputs may be any that keep to these rules, and one draw needn't show every extreme that they name: `block_links`: in each row the 2 entries are distinct and differ from the row's own block index (the second index). `stiffness`: in slot 0 every diagonal entry lies between 4 and 8. `mass_tiles`: every diagonal entry lies between 0.5 and 1.
All inputs are finite; a program needn't handle non-finite values.
Results may differ from a plain program's by a relative error of at most 0.0003.
Values sent between devices are 32-bit elements; how exact they have to be, the bound alone decides.
A program may use at most 64 MiB of HBM per device.

v0:
```python
import math

import jax
import jax.numpy as jnp
from jax import lax
from jax.sharding import PartitionSpec as P

DIRS = 3
BLOCK = 128
ITERS = 2


OMEGA_SQUARED = 0.05
SMOOTHING = 0.1
FULL_PRECISION = lax.Precision.HIGHEST


def padded(cells, sides, width):
    for axis, dim in sides:
        count = lax.axis_size(axis)
        head = lax.slice_in_dim(cells, 0, width, axis=dim)
        tail = lax.slice_in_dim(cells, cells.shape[dim] - width, cells.shape[dim], axis=dim)
        cells = jnp.concatenate(
            [
                lax.ppermute(tail, axis, [(i, (i + 1) % count) for i in range(count)]),
                cells,
                lax.ppermute(head, axis, [((i + 1) % count, i) for i in range(count)]),
            ],
            axis=dim,
        )
    return cells


def harmonic_orders(coeff_count):
    row_index = jnp.arange(coeff_count, dtype=jnp.int32)
    return (row_index + 1) // 2


def synthesis_table(first_sample, sample_count, total_samples, coeff_count):
    samples_here = first_sample + jnp.arange(sample_count, dtype=jnp.int32)
    orders = harmonic_orders(coeff_count)
    phases = samples_here[:, None] * orders[None, :] % total_samples
    angles = phases.astype(jnp.float32) * (2.0 * math.pi / total_samples)
    row_index = jnp.arange(coeff_count, dtype=jnp.int32)
    is_sine = (row_index % 2 == 0) & (row_index > 0)
    return jnp.where(is_sine[None, :], jnp.sin(angles), jnp.cos(angles))


def analysis_table(synthesis, coeff_count, total_samples):
    orders = harmonic_orders(coeff_count)
    scaling = jnp.where(orders == 0, 1.0, 2.0) / total_samples
    return synthesis * scaling[None, :]


def contact_law(motion, states, preload, normal_stiff, tangent_stiff, friction):
    normal_part = preload + normal_stiff * motion[:, 0]
    slide_one = motion[:, 1]
    slide_two = motion[:, 2]
    magnitude = jnp.sqrt(slide_one * slide_one + slide_two * slide_two + SMOOTHING * SMOOTHING)
    touching = states > 0
    sticking = states == 1
    normal_force = jnp.where(touching, normal_part, 0.0)
    slip_factor = friction * normal_force / magnitude
    tangent_factor = jnp.where(sticking, tangent_stiff, slip_factor)
    tangent_factor = jnp.where(touching, tangent_factor, 0.0)
    return jnp.stack([normal_force, tangent_factor * slide_one, tangent_factor * slide_two], axis=1)


def block_view(coeff_field):
    coeff_count, direction_count, node_count = coeff_field.shape
    divided = coeff_field.reshape(coeff_count, direction_count, node_count // BLOCK, BLOCK)
    return divided.transpose(2, 0, 1, 3).reshape(
        node_count // BLOCK, coeff_count, direction_count * BLOCK
    )


def field_view(blocks):
    block_count, coeff_count, block_width = blocks.shape
    divided = blocks.reshape(block_count, coeff_count, DIRS, BLOCK)
    return divided.transpose(1, 2, 0, 3).reshape(coeff_count, DIRS, block_count * BLOCK)


def coupled_update(
    own_field, zone_coeffs, sectors, stiffness, mass_tiles, block_links, forces, own_loads
):
    orders = harmonic_orders(own_field.shape[0]).astype(jnp.float32)
    inertia = OMEGA_SQUARED * orders * orders
    own_blocks = block_view(own_field)
    zone_blocks = block_view(zone_coeffs)
    before_blocks = block_view(sectors[:, :, 0, :])
    after_blocks = block_view(sectors[:, :, 2, :])
    linked = zone_blocks[block_links]
    sources = jnp.concatenate(
        [own_blocks[:, None], before_blocks[:, None], after_blocks[:, None], linked], axis=1
    )
    elastic = jnp.einsum(
        "bshi,bsij->bhj", sources, stiffness.astype(jnp.float32), precision=FULL_PRECISION
    )
    kinetic = jnp.einsum(
        "bhi,bij->bhj", own_blocks, mass_tiles.astype(jnp.float32), precision=FULL_PRECISION
    )
    coupled = elastic - inertia[None, :, None] * kinetic
    residual = field_view(coupled) + forces - own_loads
    stiff_diag = jnp.diagonal(stiffness[:, 0].astype(jnp.float32), axis1=-2, axis2=-1)
    mass_diag = jnp.diagonal(mass_tiles.astype(jnp.float32), axis1=-2, axis2=-1)
    pivots = stiff_diag[:, None, :] - inertia[None, :, None] * mass_diag[:, None, :]
    return (residual, own_field - residual / field_view(pivots))


def per_device(
    initial_guess,
    harmonic_loads,
    stiffness,
    mass_tiles,
    block_links,
    states,
    preload,
    normal_stiff,
    tangent_stiff,
    friction,
):
    coeff_count = initial_guess.shape[0]
    samples_dev = states.shape[0]
    total_samples = samples_dev * lax.axis_size("tm")
    own_field = initial_guess[:, :, 0, :]
    own_loads = harmonic_loads[:, :, 0, :]
    zone_states = states[:, 0, :]
    zone_preload = preload[0]
    zone_normal = normal_stiff[0]
    zone_tangent = tangent_stiff[0]
    zone_friction = friction[0]
    local_stiffness = stiffness[0]
    local_mass = mass_tiles[0]
    local_links = block_links[0]
    synthesis = synthesis_table(
        lax.axis_index("tm") * samples_dev, samples_dev, total_samples, coeff_count
    )
    analysis = analysis_table(synthesis, coeff_count, total_samples)
    residual = own_field
    for iteration in range(ITERS):
        zone_coeffs = lax.all_gather(own_field, "tm", axis=2, tiled=True)
        sectors = padded(own_field[:, :, None, :], (("zone", 2),), 1)
        motion = jnp.einsum("th,hdn->tdn", synthesis, zone_coeffs, precision=FULL_PRECISION)
        forces_time = contact_law(
            motion, zone_states, zone_preload, zone_normal, zone_tangent, zone_friction
        )
        partial_terms = jnp.einsum("th,tdn->hdn", analysis, forces_time, precision=FULL_PRECISION)
        forces = lax.psum_scatter(partial_terms, "tm", scatter_dimension=2, tiled=True)
        residual, own_field = coupled_update(
            own_field,
            zone_coeffs,
            sectors,
            local_stiffness,
            local_mass,
            local_links,
            forces,
            own_loads,
        )
    return (own_field[:, :, None, :], residual[:, :, None, :])


def solution(mesh):
    return jax.shard_map(
        per_device,
        mesh=mesh,
        in_specs=(
            P(None, None, "zone", "tm"),
            P(None, None, "zone", "tm"),
            P("zone", "tm", None, None, None),
            P("zone", "tm", None, None),
            P("zone", "tm", None),
            P("tm", "zone", None),
            P("zone", None),
            P("zone", None),
            P("zone", None),
            P("zone", None),
        ),
        out_specs=(P(None, None, "zone", "tm"), P(None, None, "zone", "tm")),
        check_vma=False,
    )
```

profile of v0, /device:TPU:0, one launch (start us, length us, event | category | flops | bytes accessed | tf_op | source)
XLA Modules:
  0.0 127.1 jit_solution(10812076237233174816)
XLA Ops:
  7.3 3.0 %collective-permute-start = (f32[15,3,1,128]{3,2,1,0:T(1,128)}, f32[15,3,1,128]{3,2,1,0:T(1,128)}, u32[]{:S(2)}, u32[]{:S(2)}) collective-permute-start(f32[15,3,1,128]{3,2,1,0:T(1,128)} %param.10), channel_id=1, source_target_pairs={{0,1},{1,2},{2,3},{3,0},{4,5},{5,6},{6,7},{7,4},{8,9},{9,10},{10,1... | collective-permute-start | bytes 69128 | tf_op jit(solution)/shard_map/ppermute | solution.py:25
  10.3 1.0 collective-permute-start.1
  11.3 0.8 copy.41
  12.1 14.8 %all-gather = f32[15,3,1,1024]{3,0,1,2:T(8,128)S(1)} all-gather(f32[15,3,1,128]{3,0,1,2:T(8,128)S(1)} %copy.41), channel_id=2, replica_groups=mesh['tm'=8,'zone'=4] {'tm'}, dimensions={3}, use_global_device_ids=true | all-gather | bytes 207360 | tf_op jit(solution)/shard_map/all_gather | solution.py:141
  26.9 2.8 %fusion.35 = f32[256,3,1024]{2,0,1:T(8,128)S(1)} fusion(f32[15,3,1,1024]{3,0,1,2:T(8,128)S(1)} %all-gather, s32[15]{0:T(128)S(1)} %and_select_fusion.1, s32[256]{0:T(256)S(1)} %iota_add_fusion, pred[15]{0:T(512)(128)(4,1)S(1)} %compare_and_fusion), kind=kOutput, calls=%fused_computation.45 | convolution fusion | flops 141615360 | bytes 3331147 | tf_op jit(solution)/shard_map/th,hdn->tdn/dot_general | solution.py:143
  29.7 0.8 fusion.31
  30.5 0.5 fusion.30
  31.2 2.4 %fusion = f32[15,3,1024]{2,0,1:T(8,128)} fusion(f32[256,1,1024]{2,0,1:T(8,128)S(1)} %fusion.30, f32[256,1,1024]{2,0,1:T(8,128)S(1)} %get-tuple-element.12, f32[256,1,1024]{2,0,1:T(8,128)S(1)} %get-tuple-element.13, f32[15]{0:T(128)S(1)} %fusion.63, s32[15]{0:T(128)S(1)} %and_select_fusion.1, s32[256]{0:T(256)S(1)} %iota_add_fusion, ...), kind=kOutput, calls=%fused_computation.4 | convolution fusion | flops 143192064 | bytes 3331207 | tf_op jit(solution)/shard_map/th,tdn->hdn/dot_general | solution.py:147
  33.7 0.6 pad_clamp_fusion
  34.3 0.7 copy_bitcast_fusion.1
  35.1 0.6 multiply_multiply_fusion
  35.7 1.6 %copy.44 = f32[8,15,384]{2,1,0:T(8,128)} copy(f32[8,15,384]{2,0,1:T(8,128)} %copy_bitcast_fusion.1) | data formatting | bytes 368640 | tf_op jit(solution)/shard_map/reshape | solution.py:72
  37.4 4.6 %gather_fusion.1 = f32[384]{0:T(512)} fusion(f32[384,384]{1,0:T(8,128)S(1)} %fusion.32, s32[384]{0:T(512)S(1)} %or_reduce_fusion), kind=kCustom, calls=%fused_computation.1 | custom fusion | bytes 6144 | tf_op jit(solution)/shard_map/jit(diagonal)/gather | solution.py:104
  42.0 3.4 %gather_fusion.2 = f32[384]{0:T(512)S(1)} fusion(f32[384,384]{1,0:T(8,128)S(1)} %bitcast_convert_fusion, s32[384]{0:T(512)S(1)} %or_reduce_fusion), kind=kCustom, calls=%fused_computation.2 | custom fusion | bytes 6144 | tf_op jit(solution)/shard_map/jit(diagonal)/gather | solution.py:105
  45.5 1.6 %gather_fusion = f32[2,15,384]{2,1,0:T(8,128)S(1)} fusion(f32[8,15,384]{2,1,0:T(8,128)} %copy.44, s32[1024]{0:T(1024)} %pad_clamp_fusion), kind=kCustom, calls=%fused_computation | custom fusion | bytes 92168 | tf_op jit(solution)/shard_map/gather | solution.py:92
  47.1 0.7 copy.46
  47.9 0.7 copy.47
  48.6 0.7 fusion.16
  49.6 14.5 %reduce-scatter.3.cloned.1.call-done = f32[15,3,128]{2,0,1:T(8,128)} async-done(((f32[15,3,1024]{2,0,1:T(8,128)}), f32[15,3,128]{2,0,1:T(8,128)}) %reduce-scatter.3.cloned.1.call-update) | async-done | bytes 23056 | tf_op jit(solution)/shard_map/reduce_scatter | solution.py:148
  64.1 0.8 fusion.50
  64.9 2.4 %collective-permute-start.3 = (f32[15,3,1,128]{3,0,1,2:T(8,128)S(1)}, f32[15,3,1,128]{3,0,1,2:T(8,128)S(1)}, u32[]{:S(2)}, u32[]{:S(2)}) collective-permute-start(f32[15,3,1,128]{3,0,1,2:T(8,128)S(1)} %bitcast.104), channel_id=1, source_target_pairs={{1,0},{2,1},{3,2},{0,3},{5,4},{6,5},{7,6},{4,7},{9,8},{10,9},{11,1... | collective-permute-start | bytes 69128 | tf_op jit(solution)/shard_map/ppermute | solution.py:27
  67.3 14.3 %all_gather.7 = f32[15,3,1024]{2,0,1:T(8,128)S(1)} all-gather(f32[15,3,128]{2,0,1:T(8,128)S(1)} %fusion.50), channel_id=1, replica_groups=mesh['tm'=8,'zone'=4] {'tm'}, dimensions={2}, use_global_device_ids=true | all-gather | bytes 207360 | tf_op jit(solution)/shard_map/all_gather | solution.py:141
  81.6 2.8 %fusion.54 = f32[256,3,1024]{2,0,1:T(8,128)S(1)} fusion(f32[15,3,1024]{2,0,1:T(8,128)S(1)} %all_gather.7, s32[15]{0:T(128)S(1)} %copy-done.18, s32[256]{0:T(256)S(1)} %copy-done.16, pred[15]{0:T(512)(128)(4,1)S(1)} %copy-done.20), kind=kOutput, calls=%fused_computation.79 | convolution fusion | flops 141615360 | bytes 3331147 | tf_op jit(solution)/shard_map/th,hdn->tdn/dot_general | solution.py:143
  84.5 0.7 fusion.29
  85.2 0.5 fusion.28
  85.8 2.4 %fusion.6 = f32[15,3,1024]{2,0,1:T(8,128)} fusion(f32[256,1,1024]{2,0,1:T(8,128)S(1)} %fusion.28, f32[256,1,1024]{2,0,1:T(8,128)S(1)} %get-tuple-element.10, f32[256,1,1024]{2,0,1:T(8,128)S(1)} %get-tuple-element.11, f32[15]{0:T(128)S(1)} %copy-done.23, s32[15]{0:T(128)S(1)} %copy-done.18, s32[256]{0:T(256)S(1)} %copy-done.16, pred[15]{0:T(512)(128)(4,1)S(1)} %copy-done.20), kind=kOutput, calls=%fused_computation.10 | convolution fusion | flops 143192064 | bytes 3331207 | tf_op jit(solution)/shard_map/th,tdn->hdn/dot_general | solution.py:147
  88.3 0.7 gather_fusion.3
  89.1 0.7 fusion.19
  90.1 28.1 %reduce-scatter.5.cloned.1.call-done = f32[15,3,128]{2,0,1:T(8,128)} async-done(((f32[15,3,1024]{2,0,1:T(8,128)}), f32[15,3,128]{2,0,1:T(8,128)}) %reduce-scatter.5.cloned.1.call-update) | async-done | bytes 23056 | tf_op jit(solution)/shard_map/reduce_scatter | solution.py:148
  118.2 0.8 subtract_bitcast_fusion
  119.0 0.6 copy.61
  119.7 0.6 copy.62
  (85 shorter events, 1.3 us)
Async XLA Ops:
  7.2 22.5 %copy-start.5 = (f32[1,1024]{1,0:T(1,128)S(1)}, f32[1,1024]{1,0:T(1,128)}, u32[]{:S(2)}) copy-start(f32[1,1024]{1,0:T(1,128)} %param.19) | copy-start | bytes 12292
  7.2 22.5 %copy-start.7 = (f32[1,1024]{1,0:T(1,128)S(1)}, f32[1,1024]{1,0:T(1,128)}, u32[]{:S(2)}) copy-start(f32[1,1024]{1,0:T(1,128)} %param.18) | copy-start | bytes 12292
  7.2 22.5 %copy-start.10 = (f32[1,1024]{1,0:T(1,128)S(1)}, f32[1,1024]{1,0:T(1,128)}, u32[]{:S(2)}) copy-start(f32[1,1024]{1,0:T(1,128)} %param.17) | copy-start | bytes 12292
  7.2 22.5 %copy-start.12 = (f32[1,1024]{1,0:T(1,128)S(1)}, f32[1,1024]{1,0:T(1,128)}, u32[]{:S(2)}) copy-start(f32[1,1024]{1,0:T(1,128)} %param.16) | copy-start | bytes 12292
  7.2 22.5 %copy-start.2 = (s32[256,1,1024]{2,1,0:T(1,128)S(1)}, s32[256,1,1024]{2,1,0:T(1,128)}, u32[]{:S(2)}) copy-start(s32[256,1,1024]{2,1,0:T(1,128)} %param.15) | copy-start | bytes 3145732
  7.2 56.8 %reduce-scatter.3.cloned.1.call-start = ((), (), s32[]{:S(2)}) async-start(), calls=%async_computation.2 | async-start | bytes 221184 | tf_op jit(solution)/shard_map/reduce_scatter | solution.py:148
  7.3 39.9 %collective-permute-start = (f32[15,3,1,128]{3,2,1,0:T(1,128)}, f32[15,3,1,128]{3,2,1,0:T(1,128)}, u32[]{:S(2)}, u32[]{:S(2)}) collective-permute-start(f32[15,3,1,128]{3,2,1,0:T(1,128)} %param.10), channel_id=1, source_target_pairs={{0,1},{1,2},{2,3},{3,0},{4,5},{5,6},{6,7},{7,4},{8,9},{9,10},{10,1... | collective-permute-start | bytes 69128 | tf_op jit(solution)/shard_map/ppermute | solution.py:25
  10.3 37.6 %collective-permute-start.1 = (f32[15,3,1,128]{3,2,1,0:T(1,128)}, f32[15,3,1,128]{3,2,1,0:T(1,128)}, u32[]{:S(2)}, u32[]{:S(2)}) collective-permute-start(f32[15,3,1,128]{3,2,1,0:T(1,128)} %param.10), channel_id=1, source_target_pairs={{1,0},{2,1},{3,2},{0,3},{5,4},{6,5},{7,6},{4,7},{9,8},{10,9},{11,1... | collective-permute-start | bytes 69128 | tf_op jit(solution)/shard_map/ppermute | solution.py:27
  11.3 19.8 %copy-start.17 = (s32[15]{0:T(128)}, s32[15]{0:T(128)S(1)}, u32[]{:S(2)}) copy-start(s32[15]{0:T(128)S(1)} %and_select_fusion.1) | copy-start | bytes 184
  11.3 19.8 %copy-start.19 = (pred[15]{0:T(512)(128)(4,1)}, pred[15]{0:T(512)(128)(4,1)S(1)}, u32[]{:S(2)}) copy-start(pred[15]{0:T(512)(128)(4,1)S(1)} %compare_and_fusion) | copy-start | bytes 49
  11.3 19.8 %copy-start.22 = (f32[15]{0:T(128)}, f32[15]{0:T(128)S(1)}, u32[]{:S(2)}) copy-start(f32[15]{0:T(128)S(1)} %fusion.63) | copy-start | bytes 184
  12.1 19.1 %copy-start.15 = (s32[256]{0:T(256)}, s32[256]{0:T(256)S(1)}, u32[]{:S(2)}) copy-start(s32[256]{0:T(256)S(1)} %iota_add_fusion) | copy-start | bytes 3076
  31.1 2.6 %copy-start.21 = (s32[1,1,2]{2,1,0:T(1,128)S(1)}, s32[1,1,2]{2,1,0:T(1,128)}, u32[]{:S(2)}) copy-start(s32[1,1,2]{2,1,0:T(1,128)} %param.14) | copy-start | bytes 28
  31.1 3.9 %copy-start = (bf16[1,1,5,384,384]{4,3,2,1,0:T(8,128)(2,1)S(1)}, bf16[1,1,5,384,384]{4,3,2,1,0:T(8,128)(2,1)}, u32[]{:S(2)}) copy-start(bf16[1,1,5,384,384]{4,3,2,1,0:T(8,128)(2,1)} %param.12) | copy-start | bytes 4423684
  31.1 3.9 %copy-start.1 = (bf16[1,1,384,384]{3,2,1,0:T(8,128)(2,1)S(1)}, bf16[1,1,384,384]{3,2,1,0:T(8,128)(2,1)}, u32[]{:S(2)}) copy-start(bf16[1,1,384,384]{3,2,1,0:T(8,128)(2,1)} %param.13) | copy-start | bytes 884740
  31.2 4.5 %copy-start.3 = (f32[15,3,1,128]{3,2,1,0:T(1,128)S(1)}, f32[15,3,1,128]{3,2,1,0:T(1,128)}, u32[]{:S(2)}) copy-start(f32[15,3,1,128]{3,2,1,0:T(1,128)} %param.10) | copy-start | bytes 69124
  33.6 84.7 %reduce-scatter.5.cloned.1.call-start = ((), (), s32[]{:S(2)}) async-start(), calls=%async_computation.3 | async-start | bytes 221184 | tf_op jit(solution)/shard_map/reduce_scatter | solution.py:148
  42.0 7.3 %copy-start.14 = (f32[15]{0:T(128)S(1)}, f32[15]{0:T(128)}, u32[]{:S(2)}) copy-start(f32[15]{0:T(128)} %multiply_multiply_fusion) | copy-start | bytes 184
  42.0 22.1 %copy-start.4 = (f32[15,3,1,128]{3,2,1,0:T(1,128)S(1)}, f32[15,3,1,128]{3,2,1,0:T(1,128)}, u32[]{:S(2)}) copy-start(f32[15,3,1,128]{3,2,1,0:T(1,128)} %param.11) | copy-start | bytes 69124
  42.0 22.1 %copy-start.9 = (f32[384]{0:T(512)S(1)}, f32[384]{0:T(512)}, u32[]{:S(2)}) copy-start(f32[384]{0:T(512)} %gather_fusion.1) | copy-start | bytes 4612
  42.0 39.7 %copy-start.16 = (s32[256]{0:T(256)S(1)}, s32[256]{0:T(256)}, u32[]{:S(2)}) copy-start(s32[256]{0:T(256)} %copy-done.15) | copy-start | bytes 3076
  42.0 39.7 %copy-start.18 = (s32[15]{0:T(128)S(1)}, s32[15]{0:T(128)}, u32[]{:S(2)}) copy-start(s32[15]{0:T(128)} %copy-done.17) | copy-start | bytes 184
  42.0 39.7 %copy-start.20 = (pred[15]{0:T(512)(128)(4,1)S(1)}, pred[15]{0:T(512)(128)(4,1)}, u32[]{:S(2)}) copy-start(pred[15]{0:T(512)(128)(4,1)} %copy-done.19) | copy-start | bytes 49
  45.4 39.0 %copy-start.6 = (f32[1,1024]{1,0:T(1,128)S(1)}, f32[1,1024]{1,0:T(1,128)}, u32[]{:S(2)}) copy-start(f32[1,1024]{1,0:T(1,128)} %param.19) | copy-start | bytes 12292
  45.5 39.0 %copy-start.8 = (f32[1,1024]{1,0:T(1,128)S(1)}, f32[1,1024]{1,0:T(1,128)}, u32[]{:S(2)}) copy-start(f32[1,1024]{1,0:T(1,128)} %param.18) | copy-start | bytes 12292
  45.5 39.0 %copy-start.11 = (f32[1,1024]{1,0:T(1,128)S(1)}, f32[1,1024]{1,0:T(1,128)}, u32[]{:S(2)}) copy-start(f32[1,1024]{1,0:T(1,128)} %param.17) | copy-start | bytes 12292
  45.5 39.0 %copy-start.13 = (f32[1,1024]{1,0:T(1,128)S(1)}, f32[1,1024]{1,0:T(1,128)}, u32[]{:S(2)}) copy-start(f32[1,1024]{1,0:T(1,128)} %param.16) | copy-start | bytes 12292
  64.9 24.1 %collective-permute-start.3 = (f32[15,3,1,128]{3,0,1,2:T(8,128)S(1)}, f32[15,3,1,128]{3,0,1,2:T(8,128)S(1)}, u32[]{:S(2)}, u32[]{:S(2)}) collective-permute-start(f32[15,3,1,128]{3,0,1,2:T(8,128)S(1)} %bitcast.104), channel_id=1, source_target_pairs={{1,0},{2,1},{3,2},{0,3},{5,4},{6,5},{7,6},{4,7},{9,8},{10,9},{11,1... | collective-permute-start | bytes 69128 | tf_op jit(solution)/shard_map/ppermute | solution.py:27
  67.3 21.7 %collective-permute-start.2 = (f32[15,3,1,128]{3,0,1,2:T(8,128)S(1)}, f32[15,3,1,128]{3,0,1,2:T(8,128)S(1)}, u32[]{:S(2)}, u32[]{:S(2)}) collective-permute-start(f32[15,3,1,128]{3,0,1,2:T(8,128)S(1)} %bitcast.105), channel_id=1, source_target_pairs={{0,1},{1,2},{2,3},{3,0},{4,5},{5,6},{6,7},{7,4},{8,9},{9,10},{10,1... | collective-permute-start | bytes 69128 | tf_op jit(solution)/shard_map/ppermute | solution.py:25
  85.2 0.6 copy-start.23
Sparse Core Ops, SparseCore 0:
  33.7 30.3 reduce-scatter.2
  89.1 29.0 reduce-scatter.4
where the time goes:
time: 128 us; the launch traced here: 127 us
  waiting for transfers between devices  42.6 us (33%)
  blocking collectives  29.1 us (23%)
  local copies, waits for them, and re-layouts  16.6 us (13%)
  between operations  14.6 us (11%)
  matrix products  12.2 us (10%)
  starting transfers between devices  6.54 us (5%)
  other arithmetic  5.5 us (4%)
    reduce_scatter x2, waiting for transfers between devices, per_device(): lax.psum_scatter(partial_terms, 'tm', scatter_dimension=2, tiled=True)  42.6 us
    all_gather x2, blocking collectives, per_device(): zone_coeffs = lax.all_gather(own_field, 'tm', axis=2, tiled=True)  29.1 us
    dot_general x2, matrix products, per_device(): jnp.einsum('th,hdn->tdn', synthesis, zone_coeffs, precision=FULL_PRECISION)  5.57 us
    dot_general x2, matrix products, per_device(): jnp.einsum('th,tdn->hdn', analysis, forces_time, precision=FULL_PRECISION)  4.74 us
    gather x1, local copies, waits for them, and re-layouts, coupled_update(): jnp.diagonal(stiffness[:, 0].astype(jnp.float32), axis1=-2, axis2=-1)  4.56 us
    ppermute x2, starting transfers between devices, padded(): lax.ppermute(head, axis, [((i + 1) % count, i) for i in range(count)])  3.47 us
    gather x1, local copies, waits for them, and re-layouts, coupled_update(): mass_diag = jnp.diagonal(mass_tiles.astype(jnp.float32), axis1=-2, axis2=-1)  3.45 us
    ppermute x2, starting transfers between devices, padded(): lax.ppermute(tail, axis, [(i, (i + 1) % count) for i in range(count)])  2.99 us
  transfers between devices with their start and end apart: 6, of which 2 were waited for; matrix products, arithmetic and copies ran while one was open for 25% of the time, Pallas kernels for 0%

commit v1 on v0

v1 whole, which is shorter than its diff:
```python
import functools
import math

import jax
import jax.numpy as jnp
import ml_dtypes
import numpy as np
from jax import lax
from jax.experimental import pallas as pl
from jax.experimental.pallas import tpu as pltpu
from jax.sharding import PartitionSpec as P

DIRS = 3
BLOCK = 128
ITERS = 2
ROWS = 16
WIDTH = DIRS * BLOCK
OMEGA_SQUARED = 0.05
SMOOTHING = 0.1
MESH = pl.DeviceIdType.MESH


def split_np(table):
    high = table.astype(ml_dtypes.bfloat16)
    low = (table - high.astype(np.float64)).astype(ml_dtypes.bfloat16)
    return high, low


def trig_tables(total_samples, coeff_count, parts):
    rows = np.arange(coeff_count)
    orders = (rows + 1) // 2
    phases = (np.arange(total_samples)[:, None] * orders[None, :]) % total_samples
    angles = phases * (2.0 * math.pi / total_samples)
    is_sine = (rows % 2 == 0) & (rows > 0)
    synthesis = np.zeros((total_samples, ROWS))
    synthesis[:, :coeff_count] = np.where(is_sine[None, :], np.sin(angles), np.cos(angles))
    scaling = np.zeros(ROWS)
    scaling[:coeff_count] = np.where(orders == 0, 1.0, 2.0) / total_samples
    analysis = synthesis * scaling[None, :]
    s_high, s_low = split_np(synthesis)
    a_high, a_low = split_np(analysis)
    samples = total_samples // parts
    stacked = np.concatenate([s_high, s_high, s_low], axis=1).reshape(parts, samples, 3 * ROWS)
    stacked_t = np.concatenate([a_high, a_low], axis=1).reshape(parts, samples, 2 * ROWS)
    return stacked, np.ascontiguousarray(stacked_t.transpose(0, 2, 1))


def split(values):
    high = values.astype(jnp.bfloat16)
    low = (values - high.astype(jnp.float32)).astype(jnp.bfloat16)
    return high, low


def mm(a, b):
    return jnp.dot(a, b, preferred_element_type=jnp.float32)


def xor_index(index, k):
    result = index
    bit = 1
    while bit <= k:
        if k & bit:
            result = result + bit * (1 - 2 * ((index // bit) % 2))
        bit *= 2
    return result


def kernel(
    n,
    zones,
    coeff_count,
    guess,
    loads,
    stiff_hbm,
    mass_hbm,
    links,
    states_hbm,
    preload,
    normal_stiff,
    tangent_stiff,
    friction,
    syn_hbm,
    ana_hbm,
    out_coeff,
    out_res,
    xin,
    lin,
    stiff,
    mass,
    states,
    syn,
    ana,
    field,
    load_field,
    zone_first,
    zone_second,
    near_x,
    part,
    recv,
    local_sem,
    state_sem,
    ag_send,
    ag_recv,
    near_send,
    near_recv,
    rs_send,
    rs_recv,
):
    me = lax.axis_index("tm")
    zone = lax.axis_index("zone")
    before = lax.rem(zone + zones - 1, zones)
    after = lax.rem(zone + 1, zones)
    peers = [xor_index(me, k) for k in range(n)]

    fetch_x = [
        pltpu.make_async_copy(guess.at[:, d, 0, :], xin.at[d], local_sem.at[d]) for d in range(DIRS)
    ]
    fetch_tables = [
        pltpu.make_async_copy(syn_hbm.at[me], syn, local_sem.at[3]),
        pltpu.make_async_copy(ana_hbm.at[me], ana, local_sem.at[4]),
    ]
    fetch_states = [
        pltpu.make_async_copy(states_hbm.at[:, peers[k], :], states.at[k], state_sem.at[k])
        for k in range(n)
    ]
    fetch_tiles = [
        pltpu.make_async_copy(stiff_hbm.at[0, 0], stiff, local_sem.at[5]),
        pltpu.make_async_copy(mass_hbm.at[0, 0], mass, local_sem.at[6]),
    ]
    fetch_loads = [
        pltpu.make_async_copy(loads.at[:, d, 0, :], lin.at[d], local_sem.at[7 + d])
        for d in range(DIRS)
    ]
    for copy in fetch_x + fetch_tables + fetch_states[:1] + fetch_tiles + fetch_states[1:] + fetch_loads:
        copy.start()

    barrier = pltpu.get_barrier_semaphore()
    for k in range(1, n):
        pl.semaphore_signal(barrier, inc=1, device_id=(peers[k], zone), device_id_type=MESH)
    for other in (before, after):
        pl.semaphore_signal(barrier, inc=1, device_id=(me, other), device_id_type=MESH)

    field[...] = jnp.zeros_like(field)
    load_field[...] = jnp.zeros_like(load_field)
    for copy in fetch_x:
        copy.wait()
    for d in range(DIRS):
        field[:coeff_count, d * BLOCK : (d + 1) * BLOCK] = xin[d]
    pl.semaphore_wait(barrier, n + 1)

    row_id = lax.broadcasted_iota(jnp.int32, (ROWS, WIDTH), 0)
    order = ((row_id + 1) // 2).astype(jnp.float32)
    inertia = OMEGA_SQUARED * order * order
    constant_row = (lax.broadcasted_iota(jnp.int32, (ROWS, BLOCK), 0) == 0).astype(jnp.float32)

    def partial_forces(x, k):
        b = pl.ds(peers[k], 1)
        normal_x = x[:, :BLOCK] * normal_stiff[b, :] + constant_row * preload[b, :]
        high, low = split(jnp.concatenate([normal_x, x[:, BLOCK:]], axis=1))
        motion = mm(syn[...], jnp.concatenate([high, low, high], axis=0))
        state = states[k]
        u1 = motion[:, BLOCK : 2 * BLOCK]
        u2 = motion[:, 2 * BLOCK :]
        inverse = lax.rsqrt(u1 * u1 + u2 * u2 + SMOOTHING * SMOOTHING)
        normal = jnp.where(state > 0, motion[:, :BLOCK], 0.0)
        factor = jnp.where(state == 1, tangent_stiff[b, :], friction[b, :] * normal * inverse)
        f_high, f_low = split(jnp.concatenate([normal, factor * u1, factor * u2], axis=1))
        first = mm(ana[...], f_high)
        return first[:ROWS] + first[ROWS:] + mm(ana[:ROWS, :], f_low)

    def both(x):
        return jnp.concatenate(split(x), axis=0)

    sent = []
    residual = None
    pivots = None
    far_first = list(range(n - 1, 0, -1))
    for it in range(ITERS):
        x = field[...]
        zone_x = (zone_first, zone_second)[it]
        zone_x[me] = x
        gather = {}
        for k in far_first:
            gather[k] = pltpu.make_async_remote_copy(
                src_ref=zone_x.at[me],
                dst_ref=zone_x.at[me],
                send_sem=ag_send.at[it, k],
                recv_sem=ag_recv.at[it, k],
                device_id=(peers[k], zone),
                device_id_type=MESH,
            )
            gather[k].start()
        near = []
        for side, other in enumerate((after, before)):
            copy = pltpu.make_async_remote_copy(
                src_ref=zone_x.at[me],
                dst_ref=near_x.at[it, side],
                send_sem=near_send.at[it, side],
                recv_sem=near_recv.at[it, side],
                device_id=(me, other),
                device_id_type=MESH,
            )
            copy.start()
            near.append(copy)
        if it == 0:
            for copy in fetch_tables:
                copy.wait()
            fetch_states[0].wait()
        total = partial_forces(x, 0)
        if it == 0:
            for copy in fetch_tiles + fetch_loads:
                copy.wait()
            for d in range(DIRS):
                load_field[:coeff_count, d * BLOCK : (d + 1) * BLOCK] = lin[d]
            eye = lax.broadcasted_iota(jnp.int32, (BLOCK, BLOCK), 0) == lax.broadcasted_iota(
                jnp.int32, (BLOCK, BLOCK), 1
            )

            def diagonal(load):
                return jnp.concatenate(
                    [
                        jnp.sum(
                            jnp.where(eye, load(d).astype(jnp.float32), 0.0),
                            axis=0,
                            keepdims=True,
                        )
                        for d in range(DIRS)
                    ],
                    axis=1,
                )

            def tile(d):
                return pl.ds(d * BLOCK, BLOCK)

            pivots = diagonal(lambda d: stiff[0, tile(d), tile(d)]) - inertia * diagonal(
                lambda d: mass[tile(d), tile(d)]
            )
        coupled = mm(both(x), stiff[0]) + mm(both(-inertia * x), mass[...])
        scatter = []
        for k in range(1, n):
            gather[k].wait_recv()
            if it == 0:
                fetch_states[k].wait()
            part[it, k] = partial_forces(zone_x[peers[k]], k)
            copy = pltpu.make_async_remote_copy(
                src_ref=part.at[it, k],
                dst_ref=recv.at[it, k],
                send_sem=rs_send.at[it, k],
                recv_sem=rs_recv.at[it, k],
                device_id=(peers[k], zone),
                device_id_type=MESH,
            )
            copy.start()
            scatter.append(copy)
        for side in range(2):
            near[side].wait_recv()
            coupled = coupled + mm(both(near_x[it, side]), stiff[1 + side])
        for slot in range(3, 5):
            coupled = coupled + mm(both(zone_x[links[0, 0, slot - 3]]), stiff[slot])
        total = total + coupled[:ROWS] + coupled[ROWS:] - load_field[...]
        for k, copy in enumerate(scatter):
            copy.wait_recv()
            total = total + recv[it, k + 1]
        residual = total
        field[...] = x - residual / pivots
        sent += list(gather.values()) + near + scatter

    stores = []
    for d in range(DIRS):
        lanes = pl.ds(d * BLOCK, BLOCK)
        xin[d] = field[:coeff_count, lanes]
        lin[d] = residual[:coeff_count, d * BLOCK : (d + 1) * BLOCK]
        stores.append(
            pltpu.make_async_copy(xin.at[d], out_coeff.at[:, d, 0, :], local_sem.at[d])
        )
        stores.append(
            pltpu.make_async_copy(lin.at[d], out_res.at[:, d, 0, :], local_sem.at[7 + d])
        )
    for copy in stores:
        copy.start()
    for copy in sent:
        copy.wait_send()
    for copy in stores:
        copy.wait()


def solution(mesh):
    n = mesh.shape["tm"]
    zones = mesh.shape["zone"]

    def per_device(
        initial_guess,
        harmonic_loads,
        stiffness,
        mass_tiles,
        block_links,
        states,
        preload,
        normal_stiff,
        tangent_stiff,
        friction,
    ):
        coeff_count = initial_guess.shape[0]
        samples = states.shape[0]
        slots = stiffness.shape[2]
        syn, ana = trig_tables(samples * n, coeff_count, n)
        hbm = pl.BlockSpec(memory_space=pltpu.HBM)
        vmem = pl.BlockSpec(memory_space=pltpu.VMEM)
        smem = pl.BlockSpec(memory_space=pltpu.SMEM)
        f32, bf16 = jnp.float32, jnp.bfloat16
        dma = pltpu.SemaphoreType.DMA
        out = jax.ShapeDtypeStruct(initial_guess.shape, f32)
        flat = [a.reshape(n, BLOCK) for a in (preload, normal_stiff, tangent_stiff, friction)]
        return pl.pallas_call(
            functools.partial(kernel, n, zones, coeff_count),
            out_shape=(out, out),
            in_specs=[hbm, hbm, hbm, hbm, smem, hbm, vmem, vmem, vmem, vmem, hbm, hbm],
            out_specs=(hbm, hbm),
            scratch_shapes=[
                pltpu.VMEM((DIRS, coeff_count, BLOCK), f32),
                pltpu.VMEM((DIRS, coeff_count, BLOCK), f32),
                pltpu.VMEM((slots, WIDTH, WIDTH), bf16),
                pltpu.VMEM((WIDTH, WIDTH), bf16),
                pltpu.VMEM((n, samples, BLOCK), jnp.int32),
                pltpu.VMEM((samples, 3 * ROWS), bf16),
                pltpu.VMEM((2 * ROWS, samples), bf16),
                pltpu.VMEM((ROWS, WIDTH), f32),
                pltpu.VMEM((ROWS, WIDTH), f32),
                pltpu.VMEM((n, ROWS, WIDTH), f32),
                pltpu.VMEM((n, ROWS, WIDTH), f32),
                pltpu.VMEM((ITERS, 2, ROWS, WIDTH), f32),
                pltpu.VMEM((ITERS, n, ROWS, WIDTH), f32),
                pltpu.VMEM((ITERS, n, ROWS, WIDTH), f32),
                dma((7 + DIRS,)),
                dma((n,)),
                dma((ITERS, n)),
                dma((ITERS, n)),
                dma((ITERS, 2)),
                dma((ITERS, 2)),
                dma((ITERS, n)),
                dma((ITERS, n)),
            ],
            compiler_params=pltpu.CompilerParams(
                collective_id=0, has_side_effects=True, vmem_limit_bytes=40 * 1024 * 1024
            ),
        )(
            initial_guess,
            harmonic_loads,
            stiffness,
            mass_tiles,
            block_links,
            states.reshape(samples, n, BLOCK),
            *flat,
            jnp.asarray(syn),
            jnp.asarray(ana),
        )

    return jax.shard_map(
        per_device,
        mesh=mesh,
        in_specs=(
            P(None, None, "zone", "tm"),
            P(None, None, "zone", "tm"),
            P("zone", "tm", None, None, None),
            P("zone", "tm", None, None),
            P("zone", "tm", None),
            P("tm", "zone", None),
            P("zone", None),
            P("zone", None),
            P("zone", None),
            P("zone", None),
        ),
        out_specs=(P(None, None, "zone", "tm"), P(None, None, "zone", "tm")),
        check_vma=False,
    )
```

time: 128 us -> 44.1 us (0.34)
  waiting for transfers between devices: 42.6 us -> 0 us
  Pallas kernels: 0 us -> 31.3 us
  blocking collectives: 29.1 us -> 0 us
  between operations: 14.6 us -> 0.66 us
  matrix products: 12.2 us -> 0 us
  starting transfers between devices: 6.54 us -> 0 us
  other arithmetic: 5.5 us -> 0 us
  local copies, waits for them, and re-layouts: 16.6 us -> 11.6 us
    reduce_scatter x2 -> x0, waiting for transfers between devices: 42.6 us -> none  [per_device(): lax.psum_scatter(partial_terms, 'tm', scatter_dimension=2, tiled=True)]
    pallas_call x0 -> x1, Pallas kernels: none -> 31.3 us  [per_device(): pl.pallas_call(functools.partial(kernel, n, zones, coeff_count), out_shap...]
    all_gather x2 -> x0, blocking collectives: 29.1 us -> none  [per_device(): zone_coeffs = lax.all_gather(own_field, 'tm', axis=2, tiled=True)]
    dot_general x8 -> x0, matrix products: 12.2 us -> none  [the longest x2 5.57 us: per_device(): jnp.einsum('th,hdn->tdn', synthesis, zone_coeffs, precision=FULL_PRECISION)]
    gather x4 -> x0, local copies, waits for them, and re-layouts: 10.3 us -> none  [the longest x1 4.56 us: coupled_update(): jnp.diagonal(stiffness[:, 0].astype(jnp.float32), axis1=-2, axis2=-1)]
    unnamed x55 -> x26, local copies, waits for them, and re-layouts: 2.28 us -> 11.6 us
    ppermute x4 -> x0, starting transfers between devices: 6.46 us -> none  [the longest x2 3.47 us: padded(): lax.ppermute(head, axis, [((i + 1) % count, i) for i in range(count)])]
    mul x5 -> x0, other arithmetic: 3.07 us -> none  [the longest x2 1.45 us: contact_law(): tangent_factor * slide_one]
  transfers between devices with their start and end apart: 6 -> 0, of which waited for: 2 -> 0; matrix products, arithmetic and copies ran while one was open for 25% -> 0% of each run, Pallas kernels for 0% -> 0%
where the time goes in v1:
time: 44.1 us; the launch traced here: 43.6 us
  Pallas kernels  31.3 us (71%)
  local copies, waits for them, and re-layouts  11.6 us (26%)
  between operations  0.66 us (1%)
    pallas_call x1, Pallas kernels, per_device(): pl.pallas_call(functools.partial(kernel, n, zones, coeff_count), out_shap...  31.3 us
    unnamed x26, local copies, waits for them, and re-layouts  11.6 us

profile of v1, /device:TPU:0, one launch (start us, length us, event | category | flops | bytes accessed | tf_op | source)
XLA Modules:
  0.0 43.6 jit_solution(11749728622634953031)
XLA Ops:
  0.6 0.0 copy-start
  0.6 1.4 %copy-done = bf16[1,1,5,384,384]{4,3,2,1,0:T(8,128)(2,1)S(1)} copy-done((bf16[1,1,5,384,384]{4,3,2,1,0:T(8,128)(2,1)S(1)}, bf16[1,1,5,384,384]{4,3,2,1,0:T(8,128)(2,1)}, u32[]{:S(2)}) %copy-start) | copy-done | bytes 1474584
  2.0 0.0 copy-start.1
  2.0 1.2 %copy-done.1 = s32[256,1,1024]{2,1,0:T(1,128)S(1)} copy-done((s32[256,1,1024]{2,1,0:T(1,128)S(1)}, s32[256,1,1024]{2,1,0:T(1,128)}, u32[]{:S(2)}) %copy-start.1) | copy-done | bytes 1048600
  3.2 0.0 copy-start.2
  3.2 1.0 %copy-done.2 = bf16[8,256,48]{2,1,0:T(8,128)(2,1)S(1)} copy-done((bf16[8,256,48]{2,1,0:T(8,128)(2,1)S(1)}, bf16[8,256,48]{2,1,0:T(8,128)(2,1)}, u32[]{:S(2)}) %copy-start.2) | copy-done | bytes 196632
  4.3 0.0 copy-start.3
  4.3 1.0 %copy-done.3 = bf16[1,1,384,384]{3,2,1,0:T(8,128)(2,1)S(1)} copy-done((bf16[1,1,384,384]{3,2,1,0:T(8,128)(2,1)S(1)}, bf16[1,1,384,384]{3,2,1,0:T(8,128)(2,1)}, u32[]{:S(2)}) %copy-start.3) | copy-done | bytes 294936
  5.2 0.0 copy-start.4
  5.2 0.9 %copy-done.4 = bf16[8,32,256]{2,1,0:T(8,128)(2,1)S(1)} copy-done((bf16[8,32,256]{2,1,0:T(8,128)(2,1)S(1)}, bf16[8,32,256]{2,1,0:T(8,128)(2,1)}, u32[]{:S(2)}) %copy-start.4) | copy-done | bytes 131096
  6.1 0.0 copy-start.5
  6.1 0.7 %copy-done.5 = f32[15,3,1,128]{3,2,1,0:T(1,128)S(1)} copy-done((f32[15,3,1,128]{3,2,1,0:T(1,128)S(1)}, f32[15,3,1,128]{3,2,1,0:T(1,128)}, u32[]{:S(2)}) %copy-start.5) | copy-done | bytes 23064
  6.9 0.0 copy-start.6
  6.9 0.7 %copy-done.6 = f32[15,3,1,128]{3,2,1,0:T(1,128)S(1)} copy-done((f32[15,3,1,128]{3,2,1,0:T(1,128)S(1)}, f32[15,3,1,128]{3,2,1,0:T(1,128)}, u32[]{:S(2)}) %copy-start.6) | copy-done | bytes 23064
  7.6 0.0 copy-start.7
  7.6 0.7 %copy-done.7 = f32[1,1024]{1,0:T(1,128)S(1)} copy-done((f32[1,1024]{1,0:T(1,128)S(1)}, f32[1,1024]{1,0:T(1,128)}, u32[]{:S(2)}) %copy-start.7) | copy-done | bytes 4120
  8.3 0.0 copy-start.8
  8.3 0.7 %copy-done.8 = f32[1,1024]{1,0:T(1,128)S(1)} copy-done((f32[1,1024]{1,0:T(1,128)S(1)}, f32[1,1024]{1,0:T(1,128)}, u32[]{:S(2)}) %copy-start.8) | copy-done | bytes 4120
  9.0 0.0 copy-start.9
  9.0 0.7 %copy-done.9 = f32[1,1024]{1,0:T(1,128)S(1)} copy-done((f32[1,1024]{1,0:T(1,128)S(1)}, f32[1,1024]{1,0:T(1,128)}, u32[]{:S(2)}) %copy-start.9) | copy-done | bytes 4120
  9.7 0.0 copy-start.10
  9.7 0.7 %copy-done.10 = f32[1,1024]{1,0:T(1,128)S(1)} copy-done((f32[1,1024]{1,0:T(1,128)S(1)}, f32[1,1024]{1,0:T(1,128)}, u32[]{:S(2)}) %copy-start.10) | copy-done | bytes 4120
  10.4 0.0 copy-start.11
  10.4 0.7 %copy-done.11 = s32[1,1,2]{2,1,0:T(1,128)S(1)} copy-done((s32[1,1,2]{2,1,0:T(1,128)S(1)}, s32[1,1,2]{2,1,0:T(1,128)}, u32[]{:S(2)}) %copy-start.11) | copy-done | bytes 32
  11.0 31.3 %shard_map.131 = (f32[15,3,1,128]{3,2,1,0:T(1,128)S(1)}, f32[15,3,1,128]{3,2,1,0:T(1,128)S(1)}) custom-call(f32[15,3,1,128]{3,2,1,0:T(1,128)S(1)} %copy-done.5, f32[15,3,1,128]{3,2,1,0:T(1,128)S(1)} %copy-done.6, bf16[1,1,5,384,384]{4,3,2,1,0:T(8,128)(2,1)S(1)} %copy-done, bf16[1,1,384,384]{3,2,1,0:T(8,128)(2,1)S(1)} %copy-done.3, ...), custom_call_target="tpu_custom_call" | custom-call | tf_op jit(solution)/shard_map/pallas_call | solution.py:314
  42.4 0.6 %copy.16 = f32[15,3,1,128]{3,2,1,0:T(1,128)} copy(f32[15,3,1,128]{3,2,1,0:T(1,128)S(1)} %get-tuple-element.4) | data formatting | bytes 46080
  43.0 0.6 %copy.17 = f32[15,3,1,128]{3,2,1,0:T(1,128)} copy(f32[15,3,1,128]{3,2,1,0:T(1,128)S(1)} %get-tuple-element.5) | data formatting | bytes 46080
Async XLA Ops:
  0.6 1.4 %copy-start = (bf16[1,1,5,384,384]{4,3,2,1,0:T(8,128)(2,1)S(1)}, bf16[1,1,5,384,384]{4,3,2,1,0:T(8,128)(2,1)}, u32[]{:S(2)}) copy-start(bf16[1,1,5,384,384]{4,3,2,1,0:T(8,128)(2,1)} %stiff_hbm.1) | copy-start | bytes 4423684
  2.0 1.2 %copy-start.1 = (s32[256,1,1024]{2,1,0:T(1,128)S(1)}, s32[256,1,1024]{2,1,0:T(1,128)}, u32[]{:S(2)}) copy-start(s32[256,1,1024]{2,1,0:T(1,128)} %param.17) | copy-start | bytes 3145732
  3.2 1.0 %copy-start.2 = (bf16[8,256,48]{2,1,0:T(8,128)(2,1)S(1)}, bf16[8,256,48]{2,1,0:T(8,128)(2,1)}, u32[]{:S(2)}) copy-start(bf16[8,256,48]{2,1,0:T(8,128)(2,1)} %constant.4.clone.syn_hbm) | copy-start | bytes 589828
  4.3 1.0 %copy-start.3 = (bf16[1,1,384,384]{3,2,1,0:T(8,128)(2,1)S(1)}, bf16[1,1,384,384]{3,2,1,0:T(8,128)(2,1)}, u32[]{:S(2)}) copy-start(bf16[1,1,384,384]{3,2,1,0:T(8,128)(2,1)} %mass_hbm.1) | copy-start | bytes 884740
  5.2 0.9 %copy-start.4 = (bf16[8,32,256]{2,1,0:T(8,128)(2,1)S(1)}, bf16[8,32,256]{2,1,0:T(8,128)(2,1)}, u32[]{:S(2)}) copy-start(bf16[8,32,256]{2,1,0:T(8,128)(2,1)} %constant.5.clone.ana_hbm) | copy-start | bytes 393220
  6.1 0.7 %copy-start.5 = (f32[15,3,1,128]{3,2,1,0:T(1,128)S(1)}, f32[15,3,1,128]{3,2,1,0:T(1,128)}, u32[]{:S(2)}) copy-start(f32[15,3,1,128]{3,2,1,0:T(1,128)} %guess.1) | copy-start | bytes 69124
  6.9 0.7 %copy-start.6 = (f32[15,3,1,128]{3,2,1,0:T(1,128)S(1)}, f32[15,3,1,128]{3,2,1,0:T(1,128)}, u32[]{:S(2)}) copy-start(f32[15,3,1,128]{3,2,1,0:T(1,128)} %loads.1) | copy-start | bytes 69124
  7.6 0.7 %copy-start.7 = (f32[1,1024]{1,0:T(1,128)S(1)}, f32[1,1024]{1,0:T(1,128)}, u32[]{:S(2)}) copy-start(f32[1,1024]{1,0:T(1,128)} %param.18) | copy-start | bytes 12292
  8.3 0.7 %copy-start.8 = (f32[1,1024]{1,0:T(1,128)S(1)}, f32[1,1024]{1,0:T(1,128)}, u32[]{:S(2)}) copy-start(f32[1,1024]{1,0:T(1,128)} %param.19) | copy-start | bytes 12292
  9.0 0.7 %copy-start.9 = (f32[1,1024]{1,0:T(1,128)S(1)}, f32[1,1024]{1,0:T(1,128)}, u32[]{:S(2)}) copy-start(f32[1,1024]{1,0:T(1,128)} %param.20) | copy-start | bytes 12292
  9.7 0.7 %copy-start.10 = (f32[1,1024]{1,0:T(1,128)S(1)}, f32[1,1024]{1,0:T(1,128)}, u32[]{:S(2)}) copy-start(f32[1,1024]{1,0:T(1,128)} %param.21) | copy-start | bytes 12292
  10.4 0.7 %copy-start.11 = (s32[1,1,2]{2,1,0:T(1,128)S(1)}, s32[1,1,2]{2,1,0:T(1,128)}, u32[]{:S(2)}) copy-start(s32[1,1,2]{2,1,0:T(1,128)} %links.1) | copy-start | bytes 28

commit v2 on v1

--- a/solution.py
+++ b/solution.py
@@ -341,7 +341,7 @@
                 dma((ITERS, n)),
             ],
             compiler_params=pltpu.CompilerParams(
-                collective_id=0, has_side_effects=True, vmem_limit_bytes=40 * 1024 * 1024
+                collective_id=0, has_side_effects=True, vmem_limit_bytes=60 * 1024 * 1024
             ),
         )(
             initial_guess,

time: 44.1 us -> 34.6 us (0.78)
  local copies, waits for them, and re-layouts: 11.6 us -> 2.7 us
    unnamed x26 -> x2, local copies, waits for them, and re-layouts: 11.6 us -> 2.7 us
where the time goes in v2:
time: 34.6 us; the launch traced here: 34.3 us
  Pallas kernels  30.9 us (89%)
  local copies, waits for them, and re-layouts  2.7 us (8%)
  between operations  0.64 us (2%)
    pallas_call x1, Pallas kernels, per_device(): pl.pallas_call(functools.partial(kernel, n, zones, coeff_count), out_shap...  30.9 us
    unnamed x2, local copies, waits for them, and re-layouts  2.7 us

profile of v2, /device:TPU:0, one launch (start us, length us, event | category | flops | bytes accessed | tf_op | source)
XLA Modules:
  0.0 34.3 jit_solution(1320577949999729932)
XLA Ops:
  0.6 30.9 %shard_map.131 = (f32[15,3,1,128]{3,2,1,0:T(1,128)}, f32[15,3,1,128]{3,2,1,0:T(1,128)}) custom-call(f32[15,3,1,128]{3,2,1,0:T(1,128)} %guess.1, f32[15,3,1,128]{3,2,1,0:T(1,128)} %loads.1, bf16[1,1,5,384,384]{4,3,2,1,0:T(8,128)(2,1)} %stiff_hbm.1, bf16[1,1,384,384]{3,2,1,0:T(8,128)(2,1)} %mass_hbm.1, s32[1,1,2]{2,1,0:T(1,128)} %links.1, ...), custom_call_target="tpu_custom_call" | custom-call | tf_op jit(solution)/shard_map/pallas_call | solution.py:314
  31.6 1.4 %copy.16 = f32[15,3,1,128]{3,2,1,0:T(1,128)} copy(f32[15,3,1,128]{3,2,1,0:T(1,128)} %get-tuple-element.4) | data formatting | bytes 46080
  32.9 1.4 %copy.17 = f32[15,3,1,128]{3,2,1,0:T(1,128)} copy(f32[15,3,1,128]{3,2,1,0:T(1,128)} %get-tuple-element.5) | data formatting | bytes 46080

commit v3 on v2

--- a/solution.py
+++ b/solution.py
@@ -105,23 +105,34 @@
     near_recv,
     rs_send,
     rs_recv,
+    fwd_send,
+    fwd_recv,
+    st_send,
+    st_recv,
 ):
     me = lax.axis_index("tm")
     zone = lax.axis_index("zone")
     before = lax.rem(zone + zones - 1, zones)
     after = lax.rem(zone + 1, zones)
-    peers = [xor_index(me, k) for k in range(n)]
+    chips = n // 2
+    chip = me // 2
+    core = me % 2
+    twin = me + 1 - 2 * core
+    peers = [2 * xor_index(chip, k) + core for k in range(chips)]
+    twins = [2 * xor_index(chip, k) + 1 - core for k in range(chips)]
 
     fetch_x = [
         pltpu.make_async_copy(guess.at[:, d, 0, :], xin.at[d], local_sem.at[d]) for d in range(DIRS)
     ]
     fetch_tables = [
-        pltpu.make_async_copy(syn_hbm.at[me], syn, local_sem.at[3]),
-        pltpu.make_async_copy(ana_hbm.at[me], ana, local_sem.at[4]),
+        pltpu.make_async_copy(syn_hbm.at[me], syn.at[0], local_sem.at[3]),
+        pltpu.make_async_copy(ana_hbm.at[me], ana.at[0], local_sem.at[4]),
+        pltpu.make_async_copy(syn_hbm.at[twin], syn.at[1], local_sem.at[7 + DIRS]),
+        pltpu.make_async_copy(ana_hbm.at[twin], ana.at[1], local_sem.at[8 + DIRS]),
     ]
     fetch_states = [
-        pltpu.make_async_copy(states_hbm.at[:, peers[k], :], states.at[k], state_sem.at[k])
-        for k in range(n)
+        pltpu.make_async_copy(states_hbm.at[:, peers[k], :], states.at[0, k], state_sem.at[k])
+        for k in range(chips)
     ]
     fetch_tiles = [
         pltpu.make_async_copy(stiff_hbm.at[0, 0], stiff, local_sem.at[5]),
@@ -135,8 +146,8 @@
         copy.start()
 
     barrier = pltpu.get_barrier_semaphore()
-    for k in range(1, n):
-        pl.semaphore_signal(barrier, inc=1, device_id=(peers[k], zone), device_id_type=MESH)
+    for peer in peers[1:] + [twin]:
+        pl.semaphore_signal(barrier, inc=1, device_id=(peer, zone), device_id_type=MESH)
     for other in (before, after):
         pl.semaphore_signal(barrier, inc=1, device_id=(me, other), device_id_type=MESH)
 
@@ -146,35 +157,48 @@
         copy.wait()
     for d in range(DIRS):
         field[:coeff_count, d * BLOCK : (d + 1) * BLOCK] = xin[d]
-    pl.semaphore_wait(barrier, n + 1)
+    pl.semaphore_wait(barrier, chips + 2)
 
     row_id = lax.broadcasted_iota(jnp.int32, (ROWS, WIDTH), 0)
     order = ((row_id + 1) // 2).astype(jnp.float32)
     inertia = OMEGA_SQUARED * order * order
     constant_row = (lax.broadcasted_iota(jnp.int32, (ROWS, BLOCK), 0) == 0).astype(jnp.float32)
 
-    def partial_forces(x, k):
+    def partial_forces(x, k, half):
         b = pl.ds(peers[k], 1)
         normal_x = x[:, :BLOCK] * normal_stiff[b, :] + constant_row * preload[b, :]
         high, low = split(jnp.concatenate([normal_x, x[:, BLOCK:]], axis=1))
-        motion = mm(syn[...], jnp.concatenate([high, low, high], axis=0))
-        state = states[k]
+        motion = mm(syn[half], jnp.concatenate([high, low, high], axis=0))
+        state = states[half, k]
         u1 = motion[:, BLOCK : 2 * BLOCK]
         u2 = motion[:, 2 * BLOCK :]
         inverse = lax.rsqrt(u1 * u1 + u2 * u2 + SMOOTHING * SMOOTHING)
         normal = jnp.where(state > 0, motion[:, :BLOCK], 0.0)
         factor = jnp.where(state == 1, tangent_stiff[b, :], friction[b, :] * normal * inverse)
         f_high, f_low = split(jnp.concatenate([normal, factor * u1, factor * u2], axis=1))
-        first = mm(ana[...], f_high)
-        return first[:ROWS] + first[ROWS:] + mm(ana[:ROWS, :], f_low)
+        first = mm(ana[half], f_high)
+        return first[:ROWS] + first[ROWS:] + mm(ana[half, :ROWS, :], f_low)
 
     def both(x):
         return jnp.concatenate(split(x), axis=0)
+
+    def to_twin(ref, index, it, k):
+        copy = pltpu.make_async_remote_copy(
+            src_ref=ref.at[index],
+            dst_ref=ref.at[index],
+            send_sem=fwd_send.at[it, k],
+            recv_sem=fwd_recv.at[it, k],
+            device_id=(twin, zone),
+            device_id_type=MESH,
+        )
+        copy.start()
+        return copy
 
     sent = []
     residual = None
     pivots = None
-    far_first = list(range(n - 1, 0, -1))
+    far_first = list(range(chips - 1, 0, -1))
+    fetch_twin = []
     for it in range(ITERS):
         x = field[...]
         zone_x = (zone_first, zone_second)[it]
@@ -190,6 +214,7 @@
                 device_id_type=MESH,
             )
             gather[k].start()
+        forward = [to_twin(zone_x, me, it, 0)]
         near = []
         for side, other in enumerate((after, before)):
             copy = pltpu.make_async_remote_copy(
@@ -203,10 +228,24 @@
             copy.start()
             near.append(copy)
         if it == 0:
+            for k in range(chips):
+                copy = pltpu.make_async_remote_copy(
+                    src_ref=states_hbm.at[:, twins[k], :],
+                    dst_ref=states.at[1, k],
+                    send_sem=st_send.at[k],
+                    recv_sem=st_recv.at[k],
+                    device_id=(twin, zone),
+                    device_id_type=MESH,
+                )
+                copy.start()
+                fetch_twin.append(copy)
             for copy in fetch_tables:
                 copy.wait()
             fetch_states[0].wait()
-        total = partial_forces(x, 0)
+        total = partial_forces(x, 0, 0)
+        if it == 0:
+            fetch_twin[0].wait_recv()
+        total = total + partial_forces(x, 0, 1)
         if it == 0:
             for copy in fetch_tiles + fetch_loads:
                 copy.wait()
@@ -237,11 +276,14 @@
             )
         coupled = mm(both(x), stiff[0]) + mm(both(-inertia * x), mass[...])
         scatter = []
-        for k in range(1, n):
+        for k in range(1, chips):
             gather[k].wait_recv()
+            forward.append(to_twin(zone_x, peers[k], it, k))
             if it == 0:
                 fetch_states[k].wait()
-            part[it, k] = partial_forces(zone_x[peers[k]], k)
+                fetch_twin[k].wait_recv()
+            arrived = zone_x[peers[k]]
+            part[it, k] = partial_forces(arrived, k, 0) + partial_forces(arrived, k, 1)
             copy = pltpu.make_async_remote_copy(
                 src_ref=part.at[it, k],
                 dst_ref=recv.at[it, k],
@@ -255,6 +297,8 @@
         for side in range(2):
             near[side].wait_recv()
             coupled = coupled + mm(both(near_x[it, side]), stiff[1 + side])
+        for copy in forward:
+            copy.wait_recv()
         for slot in range(3, 5):
             coupled = coupled + mm(both(zone_x[links[0, 0, slot - 3]]), stiff[slot])
         total = total + coupled[:ROWS] + coupled[ROWS:] - load_field[...]
@@ -263,7 +307,7 @@
             total = total + recv[it, k + 1]
         residual = total
         field[...] = x - residual / pivots
-        sent += list(gather.values()) + near + scatter
+        sent += list(gather.values()) + near + scatter + forward
 
     stores = []
     for d in range(DIRS):
@@ -278,7 +322,7 @@
         )
     for copy in stores:
         copy.start()
-    for copy in sent:
+    for copy in sent + fetch_twin:
         copy.wait_send()
     for copy in stores:
         copy.wait()
@@ -321,24 +365,28 @@
                 pltpu.VMEM((DIRS, coeff_count, BLOCK), f32),
                 pltpu.VMEM((slots, WIDTH, WIDTH), bf16),
                 pltpu.VMEM((WIDTH, WIDTH), bf16),
-                pltpu.VMEM((n, samples, BLOCK), jnp.int32),
-                pltpu.VMEM((samples, 3 * ROWS), bf16),
-                pltpu.VMEM((2 * ROWS, samples), bf16),
+                pltpu.VMEM((2, n // 2, samples, BLOCK), jnp.int32),
+                pltpu.VMEM((2, samples, 3 * ROWS), bf16),
+                pltpu.VMEM((2, 2 * ROWS, samples), bf16),
                 pltpu.VMEM((ROWS, WIDTH), f32),
                 pltpu.VMEM((ROWS, WIDTH), f32),
                 pltpu.VMEM((n, ROWS, WIDTH), f32),
                 pltpu.VMEM((n, ROWS, WIDTH), f32),
                 pltpu.VMEM((ITERS, 2, ROWS, WIDTH), f32),
-                pltpu.VMEM((ITERS, n, ROWS, WIDTH), f32),
-                pltpu.VMEM((ITERS, n, ROWS, WIDTH), f32),
-                dma((7 + DIRS,)),
-                dma((n,)),
-                dma((ITERS, n)),
-                dma((ITERS, n)),
+                pltpu.VMEM((ITERS, n // 2, ROWS, WIDTH), f32),
+                pltpu.VMEM((ITERS, n // 2, ROWS, WIDTH), f32),
+                dma((9 + DIRS,)),
+                dma((n // 2,)),
+                dma((ITERS, n // 2)),
+                dma((ITERS, n // 2)),
                 dma((ITERS, 2)),
                 dma((ITERS, 2)),
-                dma((ITERS, n)),
-                dma((ITERS, n)),
+                dma((ITERS, n // 2)),
+                dma((ITERS, n // 2)),
+                dma((ITERS, n // 2)),
+                dma((ITERS, n // 2)),
+                dma((n // 2,)),
+                dma((n // 2,)),
             ],
             compiler_params=pltpu.CompilerParams(
                 collective_id=0, has_side_effects=True, vmem_limit_bytes=60 * 1024 * 1024

time: 34.6 us -> 28.6 us (0.83)
  Pallas kernels: 30.9 us -> 25 us
    pallas_call x1, Pallas kernels: 30.9 us -> 25 us  [per_device(): pl.pallas_call(functools.partial(kernel, n, zones, coeff_count), out_shap...]
where the time goes in v3:
time: 28.6 us; the launch traced here: 28.3 us
  Pallas kernels  25 us (87%)
  local copies, waits for them, and re-layouts  2.7 us (9%)
  between operations  0.64 us (2%)
    pallas_call x1, Pallas kernels, per_device(): pl.pallas_call(functools.partial(kernel, n, zones, coeff_count), out_shap...  25 us
    unnamed x2, local copies, waits for them, and re-layouts  2.7 us

profile of v3, /device:TPU:0, one launch (start us, length us, event | category | flops | bytes accessed | tf_op | source)
XLA Modules:
  0.0 28.3 jit_solution(10015082797578094389)
XLA Ops:
  0.6 25.0 %shard_map.131 = (f32[15,3,1,128]{3,2,1,0:T(1,128)}, f32[15,3,1,128]{3,2,1,0:T(1,128)}) custom-call(f32[15,3,1,128]{3,2,1,0:T(1,128)} %guess.1, f32[15,3,1,128]{3,2,1,0:T(1,128)} %loads.1, bf16[1,1,5,384,384]{4,3,2,1,0:T(8,128)(2,1)} %stiff_hbm.1, bf16[1,1,384,384]{3,2,1,0:T(8,128)(2,1)} %mass_hbm.1, s32[1,1,2]{2,1,0:T(1,128)} %links.1, ...), custom_call_target="tpu_custom_call" | custom-call | tf_op jit(solution)/shard_map/pallas_call | solution.py:358
  25.6 1.4 %copy.16 = f32[15,3,1,128]{3,2,1,0:T(1,128)} copy(f32[15,3,1,128]{3,2,1,0:T(1,128)} %get-tuple-element.4) | data formatting | bytes 46080
  27.0 1.4 %copy.17 = f32[15,3,1,128]{3,2,1,0:T(1,128)} copy(f32[15,3,1,128]{3,2,1,0:T(1,128)} %get-tuple-element.5) | data formatting | bytes 46080

commit v4 on v3

--- a/solution.py
+++ b/solution.py
@@ -73,12 +73,12 @@
     loads,
     stiff_hbm,
     mass_hbm,
-    links,
+    links_hbm,
     states_hbm,
-    preload,
-    normal_stiff,
-    tangent_stiff,
-    friction,
+    preload_hbm,
+    normal_hbm,
+    tangent_hbm,
+    friction_hbm,
     syn_hbm,
     ana_hbm,
     out_coeff,
@@ -109,6 +109,12 @@
     fwd_recv,
     st_send,
     st_recv,
+    node_sem,
+    links,
+    preload,
+    normal_stiff,
+    tangent_stiff,
+    friction,
 ):
     me = lax.axis_index("tm")
     zone = lax.axis_index("zone")
@@ -138,11 +144,19 @@
         pltpu.make_async_copy(stiff_hbm.at[0, 0], stiff, local_sem.at[5]),
         pltpu.make_async_copy(mass_hbm.at[0, 0], mass, local_sem.at[6]),
     ]
+    fetch_nodes = [
+        pltpu.make_async_copy(preload_hbm, preload, node_sem.at[0]),
+        pltpu.make_async_copy(normal_hbm, normal_stiff, node_sem.at[1]),
+        pltpu.make_async_copy(tangent_hbm, tangent_stiff, node_sem.at[2]),
+        pltpu.make_async_copy(friction_hbm, friction, node_sem.at[3]),
+    ]
+    fetch_links = pltpu.make_async_copy(links_hbm, links, node_sem.at[4])
     fetch_loads = [
         pltpu.make_async_copy(loads.at[:, d, 0, :], lin.at[d], local_sem.at[7 + d])
         for d in range(DIRS)
     ]
-    for copy in fetch_x + fetch_tables + fetch_states[:1] + fetch_tiles + fetch_states[1:] + fetch_loads:
+    fetch_links.start()
+    for copy in fetch_x + fetch_nodes + fetch_tables + fetch_states[:1] + fetch_tiles + fetch_states[1:] + fetch_loads:
         copy.start()
 
     barrier = pltpu.get_barrier_semaphore()
@@ -239,7 +253,7 @@
                 )
                 copy.start()
                 fetch_twin.append(copy)
-            for copy in fetch_tables:
+            for copy in fetch_tables + fetch_nodes:
                 copy.wait()
             fetch_states[0].wait()
         total = partial_forces(x, 0, 0)
@@ -299,6 +313,8 @@
             coupled = coupled + mm(both(near_x[it, side]), stiff[1 + side])
         for copy in forward:
             copy.wait_recv()
+        if it == 0:
+            fetch_links.wait()
         for slot in range(3, 5):
             coupled = coupled + mm(both(zone_x[links[0, 0, slot - 3]]), stiff[slot])
         total = total + coupled[:ROWS] + coupled[ROWS:] - load_field[...]
@@ -349,8 +365,6 @@
         slots = stiffness.shape[2]
         syn, ana = trig_tables(samples * n, coeff_count, n)
         hbm = pl.BlockSpec(memory_space=pltpu.HBM)
-        vmem = pl.BlockSpec(memory_space=pltpu.VMEM)
-        smem = pl.BlockSpec(memory_space=pltpu.SMEM)
         f32, bf16 = jnp.float32, jnp.bfloat16
         dma = pltpu.SemaphoreType.DMA
         out = jax.ShapeDtypeStruct(initial_guess.shape, f32)
@@ -358,7 +372,7 @@
         return pl.pallas_call(
             functools.partial(kernel, n, zones, coeff_count),
             out_shape=(out, out),
-            in_specs=[hbm, hbm, hbm, hbm, smem, hbm, vmem, vmem, vmem, vmem, hbm, hbm],
+            in_specs=[hbm] * 12,
             out_specs=(hbm, hbm),
             scratch_shapes=[
                 pltpu.VMEM((DIRS, coeff_count, BLOCK), f32),
@@ -387,20 +401,31 @@
                 dma((ITERS, n // 2)),
                 dma((n // 2,)),
                 dma((n // 2,)),
+                dma((5,)),
+                pltpu.SMEM((1, 1, 2), jnp.int32),
+                pltpu.VMEM((n, BLOCK), f32),
+                pltpu.VMEM((n, BLOCK), f32),
+                pltpu.VMEM((n, BLOCK), f32),
+                pltpu.VMEM((n, BLOCK), f32),
             ],
             compiler_params=pltpu.CompilerParams(
-                collective_id=0, has_side_effects=True, vmem_limit_bytes=60 * 1024 * 1024
+                collective_id=0, has_side_effects=True, vmem_limit_bytes=40 * 1024 * 1024
             ),
         )(
-            initial_guess,
-            harmonic_loads,
-            stiffness,
-            mass_tiles,
-            block_links,
-            states.reshape(samples, n, BLOCK),
-            *flat,
-            jnp.asarray(syn),
-            jnp.asarray(ana),
+            *[
+                pltpu.with_memory_space_constraint(operand, pltpu.HBM)
+                for operand in (
+                    initial_guess,
+                    harmonic_loads,
+                    stiffness,
+                    mass_tiles,
+                    block_links,
+                    states.reshape(samples, n, BLOCK),
+                    *flat,
+                    jnp.asarray(syn),
+                    jnp.asarray(ana),
+                )
+            ]
         )
 
     return jax.shard_map(

time: 28.6 us -> 25.7 us (0.90)
  local copies, waits for them, and re-layouts: 2.7 us -> 1.22 us
  Pallas kernels: 25 us -> 23.7 us
    unnamed x2, local copies, waits for them, and re-layouts: 2.7 us -> 1.22 us
    pallas_call x1, Pallas kernels: 25 us -> 23.7 us  [per_device(): pl.pallas_call(functools.partial(kernel, n, zones, coeff_count), out_shap...]
where the time goes in v4:
time: 25.7 us; the launch traced here: 25.6 us
  Pallas kernels  23.7 us (92%)
  local copies, waits for them, and re-layouts  1.22 us (5%)
  between operations  0.64 us (2%)
    pallas_call x1, Pallas kernels, per_device(): pl.pallas_call(functools.partial(kernel, n, zones, coeff_count), out_shap...  23.7 us
    unnamed x2, local copies, waits for them, and re-layouts  1.22 us

profile of v4, /device:TPU:0, one launch (start us, length us, event | category | flops | bytes accessed | tf_op | source)
XLA Modules:
  0.0 25.6 jit_solution(15315940199927438352)
XLA Ops:
  0.6 23.7 %shard_map.131 = (f32[15,3,1,128]{3,2,1,0:T(1,128)S(1)}, f32[15,3,1,128]{3,2,1,0:T(1,128)S(1)}) custom-call(f32[15,3,1,128]{3,2,1,0:T(1,128)} %guess.1, f32[15,3,1,128]{3,2,1,0:T(1,128)} %loads.1, bf16[1,1,5,384,384]{4,3,2,1,0:T(8,128)(2,1)} %stiff_hbm.1, bf16[1,1,384,384]{3,2,1,0:T(8,128)(2,1)} %mass_hbm.1, s32[1,1,2]{2,1,0:T(1,128)} %links_hbm.1, ...), custom_call_target="tpu_custom_call" | custom-call | tf_op jit(solution)/shard_map/pallas_call | solution.py:372
  24.4 0.6 %copy.16 = f32[15,3,1,128]{3,2,1,0:T(1,128)} copy(f32[15,3,1,128]{3,2,1,0:T(1,128)S(1)} %get-tuple-element.4) | data formatting | bytes 46080
  25.0 0.6 %copy.17 = f32[15,3,1,128]{3,2,1,0:T(1,128)} copy(f32[15,3,1,128]{3,2,1,0:T(1,128)S(1)} %get-tuple-element.5) | data formatting | bytes 46080

commit v5 on v4

--- a/solution.py
+++ b/solution.py
@@ -325,23 +325,12 @@
         field[...] = x - residual / pivots
         sent += list(gather.values()) + near + scatter + forward
 
-    stores = []
     for d in range(DIRS):
         lanes = pl.ds(d * BLOCK, BLOCK)
-        xin[d] = field[:coeff_count, lanes]
-        lin[d] = residual[:coeff_count, d * BLOCK : (d + 1) * BLOCK]
-        stores.append(
-            pltpu.make_async_copy(xin.at[d], out_coeff.at[:, d, 0, :], local_sem.at[d])
-        )
-        stores.append(
-            pltpu.make_async_copy(lin.at[d], out_res.at[:, d, 0, :], local_sem.at[7 + d])
-        )
-    for copy in stores:
-        copy.start()
+        out_coeff[:, d, 0, :] = field[:coeff_count, lanes]
+        out_res[:, d, 0, :] = residual[:coeff_count, d * BLOCK : (d + 1) * BLOCK]
     for copy in sent + fetch_twin:
         copy.wait_send()
-    for copy in stores:
-        copy.wait()
 
 
 def solution(mesh):
@@ -373,7 +362,7 @@
             functools.partial(kernel, n, zones, coeff_count),
             out_shape=(out, out),
             in_specs=[hbm] * 12,
-            out_specs=(hbm, hbm),
+            out_specs=(pl.BlockSpec(memory_space=pltpu.VMEM),) * 2,
             scratch_shapes=[
                 pltpu.VMEM((DIRS, coeff_count, BLOCK), f32),
                 pltpu.VMEM((DIRS, coeff_count, BLOCK), f32),

time: 25.7 us -> 25.7 us (level)
  no operation moved by 1% of the time
where the time goes in v5:
time: 25.7 us; the launch traced here: 25.5 us
  Pallas kernels  23.7 us (92%)
  local copies, waits for them, and re-layouts  1.22 us (5%)
  between operations  0.64 us (2%)
    pallas_call x1, Pallas kernels, per_device(): pl.pallas_call(functools.partial(kernel, n, zones, coeff_count), out_shap...  23.7 us
    unnamed x2, local copies, waits for them, and re-layouts  1.22 us

profile of v5, /device:TPU:0, one launch (start us, length us, event | category | flops | bytes accessed | tf_op | source)
XLA Modules:
  0.0 25.5 jit_solution(15069416418680119680)
XLA Ops:
  0.6 23.7 %shard_map.131 = (f32[15,3,1,128]{3,2,1,0:T(1,128)S(1)}, f32[15,3,1,128]{3,2,1,0:T(1,128)S(1)}) custom-call(f32[15,3,1,128]{3,2,1,0:T(1,128)} %guess.1, f32[15,3,1,128]{3,2,1,0:T(1,128)} %loads.1, bf16[1,1,5,384,384]{4,3,2,1,0:T(8,128)(2,1)} %stiff_hbm.1, bf16[1,1,384,384]{3,2,1,0:T(8,128)(2,1)} %mass_hbm.1, s32[1,1,2]{2,1,0:T(1,128)} %links_hbm.1, ...), custom_call_target="tpu_custom_call" | custom-call | tf_op jit(solution)/shard_map/pallas_call | solution.py:361
  24.3 0.6 %copy.16 = f32[15,3,1,128]{3,2,1,0:T(1,128)} copy(f32[15,3,1,128]{3,2,1,0:T(1,128)S(1)} %get-tuple-element.4) | data formatting | bytes 46080
  24.9 0.6 %copy.17 = f32[15,3,1,128]{3,2,1,0:T(1,128)} copy(f32[15,3,1,128]{3,2,1,0:T(1,128)S(1)} %get-tuple-element.5) | data formatting | bytes 46080

commit v6 on v5

--- a/solution.py
+++ b/solution.py
@@ -182,16 +182,24 @@
         b = pl.ds(peers[k], 1)
         normal_x = x[:, :BLOCK] * normal_stiff[b, :] + constant_row * preload[b, :]
         high, low = split(jnp.concatenate([normal_x, x[:, BLOCK:]], axis=1))
-        motion = mm(syn[half], jnp.concatenate([high, low, high], axis=0))
-        state = states[half, k]
+        samples = syn.shape[1]
+        count = len(half) * samples
+        table = syn[half[0] : half[-1] + 1].reshape(count, 3 * ROWS)
+        motion = mm(table, jnp.concatenate([high, low, high], axis=0))
+        state = states[half[0] : half[-1] + 1, k].reshape(count, BLOCK)
         u1 = motion[:, BLOCK : 2 * BLOCK]
         u2 = motion[:, 2 * BLOCK :]
         inverse = lax.rsqrt(u1 * u1 + u2 * u2 + SMOOTHING * SMOOTHING)
         normal = jnp.where(state > 0, motion[:, :BLOCK], 0.0)
         factor = jnp.where(state == 1, tangent_stiff[b, :], friction[b, :] * normal * inverse)
         f_high, f_low = split(jnp.concatenate([normal, factor * u1, factor * u2], axis=1))
-        first = mm(ana[half], f_high)
-        return first[:ROWS] + first[ROWS:] + mm(ana[half, :ROWS, :], f_low)
+        result = None
+        for i, h in enumerate(half):
+            rows = slice(i * samples, (i + 1) * samples)
+            first = mm(ana[h], f_high[rows])
+            term = first[:ROWS] + first[ROWS:] + mm(ana[h, :ROWS, :], f_low[rows])
+            result = term if result is None else result + term
+        return result
 
     def both(x):
         return jnp.concatenate(split(x), axis=0)
@@ -256,10 +264,12 @@
             for copy in fetch_tables + fetch_nodes:
                 copy.wait()
             fetch_states[0].wait()
-        total = partial_forces(x, 0, 0)
         if it == 0:
+            total = partial_forces(x, 0, (0,))
             fetch_twin[0].wait_recv()
-        total = total + partial_forces(x, 0, 1)
+            total = total + partial_forces(x, 0, (1,))
+        else:
+            total = partial_forces(x, 0, (0, 1))
         if it == 0:
             for copy in fetch_tiles + fetch_loads:
                 copy.wait()
@@ -297,7 +307,7 @@
                 fetch_states[k].wait()
                 fetch_twin[k].wait_recv()
             arrived = zone_x[peers[k]]
-            part[it, k] = partial_forces(arrived, k, 0) + partial_forces(arrived, k, 1)
+            part[it, k] = partial_forces(arrived, k, (0, 1))
             copy = pltpu.make_async_remote_copy(
                 src_ref=part.at[it, k],
                 dst_ref=recv.at[it, k],

time: 25.7 us -> 24.9 us (0.969)
  Pallas kernels: 23.7 us -> 22.9 us
    pallas_call x1, Pallas kernels: 23.7 us -> 22.9 us  [per_device(): pl.pallas_call(functools.partial(kernel, n, zones, coeff_count), out_shap...]
where the time goes in v6:
time: 24.9 us; the launch traced here: 24.8 us
  Pallas kernels  22.9 us (92%)
  local copies, waits for them, and re-layouts  1.22 us (5%)
  between operations  0.64 us (3%)
    pallas_call x1, Pallas kernels, per_device(): pl.pallas_call(functools.partial(kernel, n, zones, coeff_count), out_shap...  22.9 us
    unnamed x2, local copies, waits for them, and re-layouts  1.22 us

profile of v6, /device:TPU:0, one launch (start us, length us, event | category | flops | bytes accessed | tf_op | source)
XLA Modules:
  0.0 24.8 jit_solution(1582973574421945271)
XLA Ops:
  0.6 22.9 %shard_map.131 = (f32[15,3,1,128]{3,2,1,0:T(1,128)S(1)}, f32[15,3,1,128]{3,2,1,0:T(1,128)S(1)}) custom-call(f32[15,3,1,128]{3,2,1,0:T(1,128)} %guess.1, f32[15,3,1,128]{3,2,1,0:T(1,128)} %loads.1, bf16[1,1,5,384,384]{4,3,2,1,0:T(8,128)(2,1)} %stiff_hbm.1, bf16[1,1,384,384]{3,2,1,0:T(8,128)(2,1)} %mass_hbm.1, s32[1,1,2]{2,1,0:T(1,128)} %links_hbm.1, ...), custom_call_target="tpu_custom_call" | custom-call | tf_op jit(solution)/shard_map/pallas_call | solution.py:371
  23.6 0.6 %copy.16 = f32[15,3,1,128]{3,2,1,0:T(1,128)} copy(f32[15,3,1,128]{3,2,1,0:T(1,128)S(1)} %get-tuple-element.4) | data formatting | bytes 46080
  24.2 0.6 %copy.17 = f32[15,3,1,128]{3,2,1,0:T(1,128)} copy(f32[15,3,1,128]{3,2,1,0:T(1,128)S(1)} %get-tuple-element.5) | data formatting | bytes 46080
